TPU v7x, 512 devices: a whole 4x8x8 slice. The times are simulated.
512 devices in a mesh: gx: 4 (over x), rest: 128 (over y, z, core).
Axes of the slice: x: 4, y: 8, z: 8, core: 2. Of those that a mesh axis runs over, the one named last changes fastest.
Arguments:
- tensor: float32 [512, 672, 672], P('rest', 'gx'), as said below
- basis: float32 [672, 128], P('gx'), may hold values from -0.25 to 0.25
Outputs:
- gram_one: float32 [672, 672], P('gx')
- core: float32 [128, 512, 672], P('gx', 'rest')
- gram_two: float32 [672, 672], replicated
Inputs may be any that keep to these rules, and one draw needn't show every extreme that they name: `tensor`: Real-valued field samples.
All inputs are finite; a program needn't handle non-finite values.
Results may differ from a plain program's by a relative error of at most 0.000073.
Values sent between devices are 32-bit elements; how exact they have to be, the bound alone decides.
No kernel may reach another device: no remote copies, remote signals or barrier semaphores. Data moves between devices by JAX's collectives and lax.ppermute only.
A program may use at most 64 MiB of HBM per device.

v0:
```python
import jax
import jax.numpy as jnp
from jax import lax
from jax.sharding import PartitionSpec as P


def local(tensor, basis):
    highest = lax.Precision.HIGHEST
    slices_here = tensor.shape[0]
    rows_here = tensor.shape[1]
    second_width = tensor.shape[2]
    slices_all = slices_here * lax.axis_size("rest")
    rank_all = basis.shape[1]
    exchanged = lax.all_to_all(tensor, "gx", split_axis=2, concat_axis=1, tiled=True)
    local_gram = jnp.einsum("kic,kjc->ij", exchanged, exchanged, precision=highest)
    summed = lax.psum(local_gram, ("gx", "rest"))
    block_rows = lax.dynamic_slice_in_dim(summed, lax.axis_index("gx") * rows_here, rows_here, 0)
    gram_one = block_rows / (slices_all * second_width)
    core = lax.psum_scatter(
        jnp.einsum("ic,kij->ckj", basis, tensor, precision=highest),
        "gx",
        scatter_dimension=0,
        tiled=True,
    )
    core_flat = core.reshape(-1, second_width)
    local_two = jnp.dot(
        core_flat.T, core_flat, precision=highest, preferred_element_type=jnp.float32
    )
    gram_sum = lax.psum(local_two, ("gx", "rest"))
    gram_two = gram_sum / (slices_all * rank_all)
    return (gram_one, core, gram_two)


def solution(mesh):
    in_specs = (P("rest", "gx", None), P("gx", None))
    out_specs = (P("gx", None), P("gx", "rest", None), P())
    return jax.shard_map(local, mesh=mesh, in_specs=in_specs, out_specs=out_specs, check_vma=False)
```

profile of v0, /device:TPU:24, one launch (start us, length us, event | category | flops | bytes accessed | tf_op | source)
XLA Modules:
  0.0 385.6 jit_solution(14953553316876162083)
XLA Ops:
  7.2 0.0 copy-start
  7.2 0.0 reduce-scatter.2.cloned.1.call-start
  7.2 0.8 copy-done
  8.1 4.3 %fusion = f32[128,4,672]{2,0,1:T(8,128)} fusion(f32[4,168,672]{2,1,0:T(8,128)} %param.2, f32[168,128]{1,0:T(8,128)S(1)} %copy-done), kind=kOutput, calls=%fused_computation.5 | convolution fusion | flops 693633024 | bytes 3268608 | tf_op jit(solution)/shard_map/ic,kij->ckj/dot_general | solution.py:20
  12.3 0.0 reduce-scatter.2.cloned.1.call-update
  12.3 0.0 all-reduce.3.cloned.1.call-start
  12.4 3.2 copy.7
  15.6 50.1 %all_to_all.18 = f32[4,168,672]{1,0,2:T(4,128)S(1)} all-to-all(f32[4,168,672]{1,0,2:T(4,128)S(1)} %copy.7), channel_id=1, replica_groups=mesh['gx'=4,'rest'=128] {'gx'}, dimensions={2} | all-to-all | bytes 3612672 | tf_op jit(solution)/shard_map/all_to_all | solution.py:14
  65.7 1.8 copy.11
  67.4 2.9 all_to_all.16
  70.3 8.9 %convolution_bitcast_fusion.1 = f32[672,672]{1,0:T(8,128)} fusion(f32[4,672,168]{1,2,0:T(8,128)} %all_to_all.16), kind=kOutput, calls=%fused_computation.2 | convolution fusion | flops 3641573376 | bytes 3612672 | tf_op jit(solution)/shard_map/kic,kjc->ij/dot_general | solution.py:15
  79.2 0.0 reduce-scatter.2.cloned.1.call-done
  79.2 4.2 %convolution_bitcast_fusion = f32[672,672]{1,0:T(8,128)} fusion(f32[32,4,672]{2,0,1:T(8,128)} %reduce-scatter.2.cloned.1.call-done), kind=kOutput, calls=%fused_computation.1 | convolution fusion | flops 693633024 | bytes 2150400 | tf_op jit(solution)/shard_map/dot_general | solution.py:26
  83.4 0.0 copy-start.1
  83.4 0.0 all-reduce.3.cloned.1.call-update
  83.5 1.0 copy-done.1
  84.4 1.0 copy.9
  85.4 288.4 %all-reduce.3.cloned.1.call-done = (f32[672,672]{1,0:T(8,128)}, f32[672,672]{1,0:T(8,128)}) async-done(((f32[672,672]{1,0:T(8,128)}, f32[672,672]{1,0:T(8,128)}), (f32[672,672]{1,0:T(8,128)}, f32[672,672]{1,0:T(8,128)})) %all-reduce.3.cloned.1.call-update) | async-done | bytes 3612688 | tf_op jit(solution)/shard_map/psum | solution.py:16
  373.9 3.0 broadcast_multiply_fusion
  376.9 1.9 dynamic-slice_multiply_fusion
Async XLA Ops:
  7.2 0.9 copy-start
  7.2 72.0 %reduce-scatter.2.cloned.1.call-start = ((), (), s32[]{:S(2)}) async-start(), calls=%async_computation.2 | async-start | bytes 1966080 | tf_op jit(solution)/shard_map/reduce_scatter | solution.py:19
  12.3 361.5 %all-reduce.3.cloned.1.call-start = ((), (), s32[]{:S(2)}) async-start(), calls=%async_computation.3 | async-start | bytes 8257536 | tf_op jit(solution)/shard_map/psum | solution.py:16
  83.4 1.0 copy-start.1
Sparse Core Ops, SparseCore 0:
  12.5 53.5 reduce-scatter.1
  83.6 290.2 all-reduce.2
where the time goes:
time: 386 us
  waiting for transfers between devices  288 us (75%)
  blocking collectives  50.1 us (13%)
  matrix products  17.4 us (5%)
  between operations  14.1 us (4%)
  local copies, waits for them, and re-layouts  10.7 us (3%)
  other arithmetic  4.89 us (1%)
    psum x1, waiting for transfers between devices, local(): summed = lax.psum(local_gram, ('gx', 'rest'))  288 us
    all_to_all x1, blocking collectives, local(): lax.all_to_all(tensor, 'gx', split_axis=2, concat_axis=1, tiled=True)  50.1 us
    dot_general x1, matrix products, local(): jnp.einsum('kic,kjc->ij', exchanged, exchanged, precision=highest)  8.86 us
  transfers between devices with their start and end apart: 2, of which 1 were waited for; matrix products, arithmetic and copies ran while one was open for 4% of the time, Pallas kernels for 0%

commit v1 on v0

--- a/solution.py
+++ b/solution.py
@@ -13,7 +13,7 @@
     rank_all = basis.shape[1]
     exchanged = lax.all_to_all(tensor, "gx", split_axis=2, concat_axis=1, tiled=True)
     local_gram = jnp.einsum("kic,kjc->ij", exchanged, exchanged, precision=highest)
-    summed = lax.psum(local_gram, ("gx", "rest"))
+    summed = lax.psum(lax.psum(local_gram, "rest"), "gx")
     block_rows = lax.dynamic_slice_in_dim(summed, lax.axis_index("gx") * rows_here, rows_here, 0)
     gram_one = block_rows / (slices_all * second_width)
     core = lax.psum_scatter(

time: 386 us -> 643 us (1.67)
  the two profiles are of different devices: /device:TPU:24 before, /device:TPU:1 now
where the time goes in v1:
time: 643 us
  waiting for transfers between devices  549 us (85%)
  blocking collectives  45.6 us (7%)
  matrix products  17.4 us (3%)
  between operations  15.7 us (2%)
  local copies, waits for them, and re-layouts  9.71 us (2%)
    psum x1, waiting for transfers between devices, local(): gram_sum = lax.psum(local_two, ('gx', 'rest'))  281 us
    psum x2, waiting for transfers between devices, local(): summed = lax.psum(lax.psum(local_gram, 'rest'), 'gx')  268 us
    all_to_all x1, blocking collectives, local(): lax.all_to_all(tensor, 'gx', split_axis=2, concat_axis=1, tiled=True)  45.6 us
  transfers between devices with their start and end apart: 4, of which 3 were waited for; matrix products, arithmetic and copies ran while one was open for 3% of the time, Pallas kernels for 0%

profile of v1, /device:TPU:1, one launch (start us, length us, event | category | flops | bytes accessed | tf_op | source)
XLA Modules:
  0.0 642.9 jit_solution(414020160427256137)
XLA Ops:
  8.0 0.0 copy-start
  8.0 0.0 reduce-scatter.2.cloned.1.call-start
  8.1 0.8 copy-done
  8.9 4.3 fusion
  13.2 0.0 reduce-scatter.2.cloned.1.call-update
  13.2 0.0 all-reduce.4.cloned.1.call-start
  13.2 3.2 copy.7
  16.4 45.6 %all_to_all.18 = f32[4,168,672]{1,0,2:T(4,128)S(1)} all-to-all(f32[4,168,672]{1,0,2:T(4,128)S(1)} %copy.7), channel_id=1, replica_groups=mesh['gx'=4,'rest'=128] {'gx'}, dimensions={2} | all-to-all | bytes 3612672 | tf_op jit(solution)/shard_map/all_to_all | solution.py:14
  62.1 1.8 copy.11
  63.8 2.9 all_to_all.16
  66.7 8.8 %convolution_bitcast_fusion.1 = f32[672,672]{1,0:T(8,128)} fusion(f32[4,672,168]{1,2,0:T(8,128)} %all_to_all.16), kind=kOutput, calls=%fused_computation.2 | convolution fusion | flops 3641573376 | bytes 3612672 | tf_op jit(solution)/shard_map/kic,kjc->ij/dot_general | solution.py:15
  75.6 0.0 all-reduce.4.cloned.1.call-update
  75.6 0.2 all-reduce.8.cloned.1.call-start
  75.8 0.0 reduce-scatter.2.cloned.1.call-done
  75.9 4.3 convolution_bitcast_fusion
  80.1 0.0 copy-start.1
  80.1 0.0 all-reduce.8.cloned.1.call-update
  80.2 0.0 all-reduce.6.cloned.1.call-start
  80.2 203.6 %all-reduce.4.cloned.1.call-done = f32[672,672]{1,0:T(8,128)} async-done(((f32[672,672]{1,0:T(8,128)}), f32[672,672]{1,0:T(8,128)}) %all-reduce.4.cloned.1.call-update) | async-done | bytes 1806352 | tf_op jit(solution)/shard_map/psum | solution.py:16
  283.8 0.0 all-reduce.6.cloned.1.call-update
  283.8 0.0 copy-done.1
  283.8 1.0 copy.9
  284.8 281.0 %all-reduce.8.cloned.1.call-done = f32[672,672]{1,0:T(8,128)} async-done(((f32[672,672]{1,0:T(8,128)}), f32[672,672]{1,0:T(8,128)}) %all-reduce.8.cloned.1.call-update) | async-done | bytes 1806352 | tf_op jit(solution)/shard_map/psum | solution.py:29
  565.8 3.0 broadcast_multiply_fusion
  568.8 64.6 %all-reduce.6.cloned.1.call-done = f32[672,672]{1,0:T(8,128)} async-done(((f32[672,672]{1,0:T(8,128)}), f32[672,672]{1,0:T(8,128)}) %all-reduce.6.cloned.1.call-update) | async-done | bytes 1806352 | tf_op jit(solution)/shard_map/psum | solution.py:16
  633.4 1.9 dynamic-slice_multiply_fusion
Async XLA Ops:
  8.0 0.9 copy-start
  8.0 67.8 %reduce-scatter.2.cloned.1.call-start = ((), (), s32[]{:S(2)}) async-start(), calls=%async_computation.4 | async-start | bytes 1966080 | tf_op jit(solution)/shard_map/reduce_scatter | solution.py:19
  13.2 270.6 %all-reduce.4.cloned.1.call-start = ((), (), s32[]{:S(2)}) async-start(), calls=%async_computation.2 | async-start | bytes 4128768 | tf_op jit(solution)/shard_map/psum | solution.py:16
  75.6 490.2 %all-reduce.8.cloned.1.call-start = ((), (), s32[]{:S(2)}) async-start(), calls=%async_computation.5 | async-start | bytes 4128768 | tf_op jit(solution)/shard_map/psum | solution.py:29
  80.1 203.7 %copy-start.1 = (f32[32,4,672]{2,0,1:T(8,128)S(1)}, f32[32,4,672]{2,0,1:T(8,128)}, u32[]{:S(2)}) copy-start(f32[32,4,672]{2,0,1:T(8,128)} %reduce-scatter.2.cloned.1.call-done) | copy-start | bytes 1032196
  80.2 553.2 %all-reduce.6.cloned.1.call-start = ((), (), s32[]{:S(2)}) async-start(), calls=%async_computation.3 | async-start | bytes 4128768 | tf_op jit(solution)/shard_map/psum | solution.py:16
Sparse Core Ops, SparseCore 0:
  13.3 54.6 reduce-scatter.1
Sparse Core Ops, SparseCore 1:
  75.7 208.0 all-reduce.3
  289.1 276.6 all-reduce.7
  568.2 65.1 all-reduce.5
